TPU v7x, 32 devices: a whole 2x2x4 slice. The times are simulated.
32 devices in a mesh: ep: 8 (over z, y), tp: 4 (over x, core).
Axes of the slice: x: 2, y: 2, z: 4, core: 2. Of those that a mesh axis runs over, the one named last changes fastest.
Arguments:
- tokens: bfloat16 [1024, 4096], P('ep', 'tp'), may hold values from -6 to 6
- out_grad: bfloat16 [1024, 4096], P('ep', 'tp'), may hold values from -6 to 6
- expert_ids: int32 [1024, 4], P('ep'), may hold values from 0 to 7, all different within a row; in each aligned block of 128 rows (0 to 127, 128 to 255, ...) at most 72 rows name the same one
- route_probs: float32 [1024, 4], P('ep'), may hold values from 0.05 to 0.5
- w_gate: bfloat16 [8, 4096, 768], P('ep', 'tp'), may hold values from -0.09375 to 0.09375
- w_up: bfloat16 [8, 4096, 768], P('ep', 'tp'), may hold values from -0.09375 to 0.09375
- w_down: bfloat16 [8, 768, 4096], P('ep', None, 'tp'), may hold values from -0.21875 to 0.21875
Outputs:
- grad_tokens: bfloat16 [1024, 4096], P('ep', 'tp')
- fisher_gate: bfloat16 [8, 4096, 768], P('ep', 'tp')
- fisher_up: bfloat16 [8, 4096, 768], P('ep', 'tp')
- fisher_down: bfloat16 [8, 768, 4096], P('ep', None, 'tp')
Inputs may be any that keep to these rules, and one draw needn't show every extreme that they name: `expert_ids`: each token names 4 different experts; among the tokens of one index of ep no expert is named by more than 72 tokens, a bound that some block reaches.
All inputs are finite; a program needn't handle non-finite values.
Results may differ from a plain program's by a relative error of at most 0.03.
Values may be sent and summed in bfloat16 or wider, within the bound.
A program may use at most 128 MiB of HBM per device.

v0:
```python
import jax
import jax.numpy as jnp
from jax import lax
from jax.sharding import PartitionSpec as P


def contract_rows(left, right):
    return lax.dot_general(
        left, right, (((0,), (0,)), ((), ())), preferred_element_type=jnp.float32
    )


def contract_cols(left, right):
    return lax.dot_general(
        left, right, (((1,), (1,)), ((), ())), preferred_element_type=jnp.float32
    )


def swiglu_back(gate, up, dact):
    sig = jax.nn.sigmoid(gate)
    act = (gate * sig * up).astype(jnp.bfloat16)
    dgate = (dact * up * sig * (1.0 + gate * (1.0 - sig))).astype(jnp.bfloat16)
    dup = (dact * gate * sig).astype(jnp.bfloat16)
    return (act, dgate, dup)


def squared(values):
    return jnp.square(values.astype(jnp.float32)).astype(jnp.bfloat16)


def on_device(tokens, out_grad, expert_ids, route_probs, w_gate, w_up, w_down):
    tok_rows = tokens.shape[0]
    width_part = tokens.shape[1]
    top_count = expert_ids.shape[1]
    experts = lax.axis_size("ep")
    capacity = tok_rows * top_count * 9 // (8 * experts)
    assigns = tok_rows * top_count
    flat_ids = expert_ids.reshape(-1)
    onehot = (flat_ids[:, None] == jnp.arange(experts, dtype=jnp.int32)[None, :]).astype(jnp.int32)
    ranks = jnp.sum((jnp.cumsum(onehot, 0) - onehot) * onehot, 1)
    slot_index = flat_ids * capacity + ranks
    table = (
        jnp.full((experts * capacity,), assigns, jnp.int32)
        .at[slot_index]
        .set(jnp.arange(assigns, dtype=jnp.int32))
    )
    token_of = table // top_count
    padded_x = jnp.concatenate([tokens, jnp.zeros((1, width_part), tokens.dtype)], 0)
    padded_dy = jnp.concatenate([out_grad, jnp.zeros((1, width_part), out_grad.dtype)], 0)
    padded_p = jnp.concatenate([route_probs.reshape(-1), jnp.zeros((1,), jnp.float32)], 0)
    send_x = padded_x[token_of].reshape(experts, capacity, width_part)
    send_dy = (padded_dy[token_of].astype(jnp.float32) * padded_p[table][:, None]).astype(
        jnp.bfloat16
    )
    send_dy = send_dy.reshape(experts, capacity, width_part)
    gate_mat = w_gate[0]
    up_mat = w_up[0]
    down_mat = w_down[0]
    recv_x, recv_dy = (
        lax.all_to_all(send_x, "ep", split_axis=0, concat_axis=0, tiled=True),
        lax.all_to_all(send_dy, "ep", split_axis=0, concat_axis=0, tiled=True),
    )
    recv_x = recv_x.reshape(-1, width_part)
    recv_dy = recv_dy.reshape(-1, width_part)
    gate_part = jnp.dot(recv_x, gate_mat, preferred_element_type=jnp.float32)
    up_part = jnp.dot(recv_x, up_mat, preferred_element_type=jnp.float32)
    dact_part = contract_cols(recv_dy, down_mat)
    gate, up, dact = (
        lax.psum(gate_part.astype(jnp.bfloat16), "tp").astype(jnp.float32),
        lax.psum(up_part.astype(jnp.bfloat16), "tp").astype(jnp.float32),
        lax.psum(dact_part.astype(jnp.bfloat16), "tp").astype(jnp.float32),
    )
    act, dgate, dup = swiglu_back(gate, up, dact)
    dx_rows = (contract_cols(dgate, gate_mat) + contract_cols(dup, up_mat)).astype(jnp.bfloat16)
    returned = lax.all_to_all(
        dx_rows.reshape(experts, capacity, width_part),
        "ep",
        split_axis=0,
        concat_axis=0,
        tiled=True,
    )
    scale = 1.0 / tok_rows
    x_sq = squared(recv_x)
    fisher_gate = (contract_rows(x_sq, squared(dgate)) * scale).astype(jnp.bfloat16)[None]
    fisher_up = (contract_rows(x_sq, squared(dup)) * scale).astype(jnp.bfloat16)[None]
    fisher_down = (contract_rows(squared(act), squared(recv_dy)) * scale).astype(jnp.bfloat16)[None]
    pulled = returned.reshape(experts * capacity, width_part)[slot_index].astype(jnp.float32)
    grad_tokens = jnp.sum(pulled.reshape(tok_rows, top_count, width_part), 1).astype(jnp.bfloat16)
    return (grad_tokens, fisher_gate, fisher_up, fisher_down)


def solution(mesh):
    in_specs = (
        P("ep", "tp"),
        P("ep", "tp"),
        P("ep", None),
        P("ep", None),
        P("ep", "tp", None),
        P("ep", "tp", None),
        P("ep", None, "tp"),
    )
    out_specs = (P("ep", "tp"), P("ep", "tp", None), P("ep", "tp", None), P("ep", None, "tp"))
    return jax.shard_map(
        on_device, mesh=mesh, in_specs=in_specs, out_specs=out_specs, check_vma=False
    )
```

profile of v0, /device:TPU:0, one launch (start us, length us, event | category | flops | bytes accessed | tf_op | source)
XLA Modules:
  0.0 202.3 jit_solution(541118483908250791)
XLA Ops:
  7.2 0.8 broadcast_multiply_fusion
  8.0 0.8 copy.12
  8.9 0.1 eq.25
  9.0 0.1 copy.11
  9.1 0.1 mul.68
  9.2 1.1 reduce-window.6
  10.4 0.2 slice_reduce_fusion
  10.7 2.4 %scatter_custom_fusion = s32[576]{0:T(1024)S(1)} fusion(s32[512]{0:T(512)S(1)} %bitcast.50, s32[512]{0:T(512)S(1)} %iota.11, s32[]{:T(128)} %constant.15.clone.1), kind=kCustom, calls=%fused_computation.68 | custom fusion | bytes 2308 | tf_op jit(solution)/shard_map/scatter | solution.py:45
  13.2 1.0 concatenate.11
  14.2 3.4 %gather_fusion.2 = bf16[576,1024]{1,0:T(8,128)(2,1)} fusion(bf16[129,1024]{1,0:T(8,128)(2,1)S(1)} %concatenate.11, s32[1024]{0:T(1024)S(1)} %get-tuple-element.10), kind=kCustom, calls=%fused_computation.2 | custom fusion | bytes 2361600 | tf_op jit(solution)/shard_map/gather | solution.py:51
  17.6 7.4 %all-to-all-start.1 = ((bf16[8,72,1024]{2,1,0:T(8,128)(2,1)}), bf16[8,72,1024]{2,1,0:T(8,128)(2,1)}, u32[]{:S(2)}, u32[]{:S(2)}) async-start(bf16[8,72,1024]{2,1,0:T(8,128)(2,1)} %bitcast.7), calls=%async_computation.1 | async-start | bytes 2359296 | tf_op jit(solution)/shard_map/all_to_all | solution.py:60
  25.1 2.9 %gather_fusion = bf16[576,1024]{1,0:T(8,128)(2,1)S(1)} fusion(bf16[129,1024]{1,0:T(8,128)(2,1)S(1)} %concatenate.9, s32[1024]{0:T(1024)S(1)} %get-tuple-element.10), kind=kCustom, calls=%fused_computation | custom fusion | bytes 2361600 | tf_op jit(solution)/shard_map/gather | solution.py:52
  28.0 0.1 copy.14
  28.2 2.6 %gather_fusion.1 = f32[576]{0:T(1024)S(1)} fusion(f32[513]{0:T(1024)S(1)} %pad_maximum_fusion, s32[1024]{0:T(1024)S(1)} %get-tuple-element.9), kind=kCustom, calls=%fused_computation.1 | custom fusion | bytes 6912 | tf_op jit(solution)/shard_map/gather | solution.py:52
  30.9 1.3 fusion
  32.2 21.6 %all-to-all-done.1 = bf16[8,72,1024]{2,1,0:T(8,128)(2,1)} async-done(((bf16[8,72,1024]{2,1,0:T(8,128)(2,1)}), bf16[8,72,1024]{2,1,0:T(8,128)(2,1)}, u32[]{:S(2)}, u32[]{:S(2)}) %all-to-all-start.1) | async-done | bytes 1179680 | tf_op jit(solution)/shard_map/all_to_all | solution.py:60
  53.8 3.6 %all-to-all-start = ((bf16[8,72,1024]{2,1,0:T(8,128)(2,1)}), bf16[8,72,1024]{2,1,0:T(8,128)(2,1)S(1)}, u32[]{:S(2)}, u32[]{:S(2)}) async-start(bf16[8,72,1024]{2,1,0:T(8,128)(2,1)} %fusion), calls=%async_computation | async-start | bytes 2359296 | tf_op jit(solution)/shard_map/all_to_all | solution.py:61
  57.4 3.8 %fusion.26 = bf16[576,768]{1,0:T(8,128)(2,1)} fusion(bf16[576,1024]{1,0:T(8,128)(2,1)} %bitcast.8, bf16[1,1024,768]{2,1,0:T(8,128)(2,1)} %param.12), kind=kOutput, calls=%fused_computation.45 | convolution fusion | flops 906412032 | bytes 3637248 | tf_op jit(solution)/shard_map/dot_general | solution.py:66
  61.2 3.3 %fusion.29 = bf16[576,768]{1,0:T(8,128)(2,1)} fusion(bf16[576,1024]{1,0:T(8,128)(2,1)} %bitcast.8, bf16[1,1024,768]{2,1,0:T(8,128)(2,1)S(1)} %copy-done), kind=kOutput, calls=%fused_computation.46 | convolution fusion | flops 906412032 | bytes 3637248 | tf_op jit(solution)/shard_map/dot_general | solution.py:65
  64.5 21.6 %all-to-all-done = bf16[8,72,1024]{2,1,0:T(8,128)(2,1)S(1)} async-done(((bf16[8,72,1024]{2,1,0:T(8,128)(2,1)}), bf16[8,72,1024]{2,1,0:T(8,128)(2,1)S(1)}, u32[]{:S(2)}, u32[]{:S(2)}) %all-to-all-start) | async-done | bytes 1179680 | tf_op jit(solution)/shard_map/all_to_all | solution.py:61
  86.1 3.9 %fusion.23 = bf16[576,768]{1,0:T(8,128)(2,1)} fusion(bf16[576,1024]{1,0:T(8,128)(2,1)S(1)} %bitcast.47, bf16[1,768,1024]{2,1,0:T(8,128)(2,1)} %param.13), kind=kOutput, calls=%fused_computation.44 | convolution fusion | flops 906412032 | bytes 3637248 | tf_op jit(solution)/shard_map/dot_general | solution.py:14
  90.0 59.7 %all-reduce.5.cloned.1.call-done = (bf16[576,768]{1,0:T(8,128)(2,1)}, bf16[576,768]{1,0:T(8,128)(2,1)}, bf16[576,768]{1,0:T(8,128)(2,1)}) async-done(((bf16[576,768]{1,0:T(8,128)(2,1)}, bf16[576,768]{1,0:T(8,128)(2,1)}, bf16[576,768]{1,0:T(8,128)(2,1)}), (bf16[576,768]{1,0:T(8,128)(2,1)}, bf16[576,768]{1,0:T(8,128)(2,1)}, bf16[576,768]{1,0:T(8,128)(2,1)})) %all-reduce.5.cloned.1.call-update) | async-done | bytes 2654224 | tf_op jit(solution)/shard_map/psum | solution.py:70
  149.7 3.3 %fusion.11 = f32[576,1024]{1,0:T(8,128)S(1)} fusion(bf16[1,1024,768]{2,1,0:T(8,128)(2,1)S(1)} %copy-done, bf16[576,768]{1,0:T(8,128)(2,1)} %get-tuple-element.4, bf16[576,768]{1,0:T(8,128)(2,1)} %get-tuple-element.5, bf16[576,768]{1,0:T(8,128)(2,1)} %get-tuple-element.6), kind=kOutput, calls=%fused_computation.32 | convolution fusion | flops 911720448 | bytes 6586368 | tf_op jit(solution)/shard_map/dot_general | solution.py:14
  153.1 2.2 %add_convert_fusion = bf16[576,1024]{1,0:T(8,128)(2,1)} fusion(f32[576,1024]{1,0:T(8,128)S(1)} %fusion.11, bf16[1,1024,768]{2,1,0:T(8,128)(2,1)S(1)} %copy-done.4, bf16[576,768]{1,0:T(8,128)(2,1)S(1)} %copy-done.8, bf16[576,768]{1,0:T(8,128)(2,1)S(1)} %copy-done.6), kind=kOutput, calls=%fused_computation.16 | convolution fusion | flops 910688256 | bytes 6881280 | tf_op jit(solution)/shard_map/dot_general | solution.py:14
  155.3 5.5 %all-to-all-start.2 = ((bf16[8,72,1024]{2,1,0:T(8,128)(2,1)}), bf16[8,72,1024]{2,1,0:T(8,128)(2,1)S(1)}, u32[]{:S(2)}, u32[]{:S(2)}) async-start(bf16[8,72,1024]{2,1,0:T(8,128)(2,1)} %bitcast.49), calls=%async_computation.2 | async-start | bytes 2359296 | tf_op jit(solution)/shard_map/all_to_all | solution.py:75
  160.9 4.8 %fusion.22 = bf16[1,768,1024]{2,1,0:T(8,128)(2,1)} fusion(bf16[576,1024]{1,0:T(8,128)(2,1)} %bitcast.48, bf16[576,768]{1,0:T(8,128)(2,1)} %get-tuple-element.4, bf16[576,768]{1,0:T(8,128)(2,1)} %get-tuple-element.6), kind=kOutput, calls=%fused_computation.43 | convolution fusion | flops 914178048 | bytes 4521984 | tf_op jit(solution)/shard_map/dot_general | solution.py:8
  165.7 4.2 %fusion.21 = bf16[1,1024,768]{2,1,0:T(8,128)(2,1)} fusion(bf16[576,1024]{1,0:T(8,128)(2,1)} %bitcast.8, bf16[576,768]{1,0:T(8,128)(2,1)S(1)} %copy-done.9, bf16[576,768]{1,0:T(8,128)(2,1)S(1)} %copy-done.7), kind=kOutput, calls=%fused_computation.42 | convolution fusion | flops 914178048 | bytes 4521984 | tf_op jit(solution)/shard_map/dot_general | solution.py:8
  169.9 4.4 %fusion.20 = bf16[1,1024,768]{2,1,0:T(8,128)(2,1)} fusion(bf16[576,1024]{1,0:T(8,128)(2,1)} %bitcast.8, bf16[576,768]{1,0:T(8,128)(2,1)S(1)} %copy-done.5, bf16[576,768]{1,0:T(8,128)(2,1)S(1)} %copy-done.7, bf16[576,768]{1,0:T(8,128)(2,1)S(1)} %copy-done.9), kind=kOutput, calls=%fused_computation.41 | convolution fusion | flops 916389888 | bytes 5406720 | tf_op jit(solution)/shard_map/dot_general | solution.py:8
  174.3 14.9 %all-to-all-done.2 = bf16[8,72,1024]{2,1,0:T(8,128)(2,1)S(1)} async-done(((bf16[8,72,1024]{2,1,0:T(8,128)(2,1)}), bf16[8,72,1024]{2,1,0:T(8,128)(2,1)S(1)}, u32[]{:S(2)}, u32[]{:S(2)}) %all-to-all-start.2) | async-done | bytes 1179680 | tf_op jit(solution)/shard_map/all_to_all | solution.py:75
  189.2 2.8 %gather_fusion.3 = bf16[512,1024]{1,0:T(8,128)(2,1)} fusion(bf16[576,1024]{1,0:T(8,128)(2,1)S(1)} %bitcast.45, s32[1024]{0:T(1024)S(1)} %pad_clamp_fusion), kind=kCustom, calls=%fused_computation.3 | custom fusion | bytes 2099200 | tf_op jit(solution)/shard_map/gather | solution.py:87
  191.9 1.5 gather.18
  193.4 2.1 %reduce_sum.25 = bf16[128,1024]{1,0:T(8,128)(2,1)} reduce(bf16[128,4,1024]{2,1,0:T(4,128)(2,1)S(1)} %gather.18, bf16[]{:T(256)} %constant.14.clone.1), dimensions={1}, to_apply=%region_7.8 | reduce | flops 393216 | bytes 1310722 | tf_op jit(solution)/shard_map/reduce_sum | solution.py:88
  (36 shorter events, 0.6 us)
Async XLA Ops:
  7.2 54.0 %copy-start = (bf16[1,1024,768]{2,1,0:T(8,128)(2,1)S(1)}, bf16[1,1024,768]{2,1,0:T(8,128)(2,1)}, u32[]{:S(2)}) copy-start(bf16[1,1024,768]{2,1,0:T(8,128)(2,1)} %param.11) | copy-start | bytes 4718596
  17.6 7.4 %copy-start.2 = (bf16[128,1024]{1,0:T(8,128)(2,1)S(1)}, bf16[128,1024]{1,0:T(8,128)(2,1)}, u32[]{:S(2)}) copy-start(bf16[128,1024]{1,0:T(8,128)(2,1)} %param.8) | copy-start | bytes 786436
  17.6 36.1 %all-to-all-start.1 = ((bf16[8,72,1024]{2,1,0:T(8,128)(2,1)}), bf16[8,72,1024]{2,1,0:T(8,128)(2,1)}, u32[]{:S(2)}, u32[]{:S(2)}) async-start(bf16[8,72,1024]{2,1,0:T(8,128)(2,1)} %bitcast.7), calls=%async_computation.1 | async-start | bytes 2359296 | tf_op jit(solution)/shard_map/all_to_all | solution.py:60
  25.1 2.9 %copy-start.3 = (f32[128,4]{0,1:T(4,128)S(1)}, f32[128,4]{0,1:T(4,128)}, u32[]{:S(2)}) copy-start(f32[128,4]{0,1:T(4,128)} %param.10) | copy-start | bytes 6148
  53.8 32.4 %all-to-all-start = ((bf16[8,72,1024]{2,1,0:T(8,128)(2,1)}), bf16[8,72,1024]{2,1,0:T(8,128)(2,1)S(1)}, u32[]{:S(2)}, u32[]{:S(2)}) async-start(bf16[8,72,1024]{2,1,0:T(8,128)(2,1)} %fusion), calls=%async_computation | async-start | bytes 2359296 | tf_op jit(solution)/shard_map/all_to_all | solution.py:61
  57.4 92.3 %all-reduce.5.cloned.1.call-start = ((), (), s32[]{:S(2)}) async-start(), calls=%async_computation.3 | async-start | bytes 5308416 | tf_op jit(solution)/shard_map/psum | solution.py:70
  86.1 3.9 %copy-start.1 = (bf16[8,72,1024]{2,1,0:T(8,128)(2,1)}, bf16[8,72,1024]{2,1,0:T(8,128)(2,1)S(1)}, u32[]{:S(2)}) copy-start(bf16[8,72,1024]{2,1,0:T(8,128)(2,1)S(1)} %all-to-all-done) | copy-start | bytes 3538948
  149.7 3.3 %copy-start.4 = (bf16[1,1024,768]{2,1,0:T(8,128)(2,1)S(1)}, bf16[1,1024,768]{2,1,0:T(8,128)(2,1)}, u32[]{:S(2)}) copy-start(bf16[1,1024,768]{2,1,0:T(8,128)(2,1)} %param.12) | copy-start | bytes 4718596
  149.7 3.4 %copy-start.6 = (bf16[576,768]{1,0:T(8,128)(2,1)S(1)}, bf16[576,768]{1,0:T(8,128)(2,1)}, u32[]{:S(2)}) copy-start(bf16[576,768]{1,0:T(8,128)(2,1)} %get-tuple-element.5) | copy-start | bytes 2654212
  149.7 3.4 %copy-start.8 = (bf16[576,768]{1,0:T(8,128)(2,1)S(1)}, bf16[576,768]{1,0:T(8,128)(2,1)}, u32[]{:S(2)}) copy-start(bf16[576,768]{1,0:T(8,128)(2,1)} %get-tuple-element.6) | copy-start | bytes 2654212
  155.3 33.8 %all-to-all-start.2 = ((bf16[8,72,1024]{2,1,0:T(8,128)(2,1)}), bf16[8,72,1024]{2,1,0:T(8,128)(2,1)S(1)}, u32[]{:S(2)}, u32[]{:S(2)}) async-start(bf16[8,72,1024]{2,1,0:T(8,128)(2,1)} %bitcast.49), calls=%async_computation.2 | async-start | bytes 2359296 | tf_op jit(solution)/shard_map/all_to_all | solution.py:75
  160.9 4.9 %copy-start.7 = (bf16[576,768]{1,0:T(8,128)(2,1)S(1)}, bf16[576,768]{1,0:T(8,128)(2,1)}, u32[]{:S(2)}) copy-start(bf16[576,768]{1,0:T(8,128)(2,1)} %get-tuple-element.5) | copy-start | bytes 2654212
  160.9 4.9 %copy-start.9 = (bf16[576,768]{1,0:T(8,128)(2,1)S(1)}, bf16[576,768]{1,0:T(8,128)(2,1)}, u32[]{:S(2)}) copy-start(bf16[576,768]{1,0:T(8,128)(2,1)} %get-tuple-element.6) | copy-start | bytes 2654212
  165.7 4.2 %copy-start.5 = (bf16[576,768]{1,0:T(8,128)(2,1)S(1)}, bf16[576,768]{1,0:T(8,128)(2,1)}, u32[]{:S(2)}) copy-start(bf16[576,768]{1,0:T(8,128)(2,1)} %get-tuple-element.4) | copy-start | bytes 2654212
Sparse Core Ops, SparseCore 0:
  90.2 59.5 all-reduce.4
where the time goes:
time: 203 us; the launch traced here: 202 us
  waiting for transfers between devices  118 us (58%)
  matrix products  29.9 us (15%)
  local copies, waits for them, and re-layouts  18.3 us (9%)
  starting transfers between devices  16.6 us (8%)
  between operations  14.2 us (7%)
  other arithmetic  5.5 us (3%)
    psum x1, waiting for transfers between devices, on_device(): lax.psum(up_part.astype(jnp.bfloat16), 'tp').astype(jnp.float32)  59.7 us
    all_to_all x1, waiting for transfers between devices, on_device(): lax.all_to_all(send_dy, 'ep', split_axis=0, concat_axis=0, tiled=True)  21.6 us
    all_to_all x1, waiting for transfers between devices, on_device(): lax.all_to_all(send_x, 'ep', split_axis=0, concat_axis=0, tiled=True)  21.6 us
    all_to_all x1, waiting for transfers between devices, on_device(): lax.all_to_all(dx_rows.reshape(experts, capacity, width_part), 'ep', spli...  14.9 us
    dot_general x3, matrix products, contract_rows(): lax.dot_general(left, right, (((0,), (0,)), ((), ())), preferred_element_...  13.4 us
    dot_general x3, matrix products, contract_cols(): lax.dot_general(left, right, (((1,), (1,)), ((), ())), preferred_element_...  9.42 us
    all_to_all x1, starting transfers between devices, on_device(): lax.all_to_all(send_x, 'ep', split_axis=0, concat_axis=0, tiled=True)  7.44 us
    all_to_all x1, starting transfers between devices, on_device(): lax.all_to_all(dx_rows.reshape(experts, capacity, width_part), 'ep', spli...  5.52 us
  transfers between devices with their start and end apart: 4, of which 4 were waited for; matrix products, arithmetic and copies ran while one was open for 14% of the time, Pallas kernels for 0%

commit v1 on v0

--- a/solution.py
+++ b/solution.py
@@ -2,6 +2,11 @@
 import jax.numpy as jnp
 from jax import lax
 from jax.sharding import PartitionSpec as P
+
+
+def add_all(x, name):
+    blocks = lax.all_gather(x, name)
+    return jnp.sum(blocks, axis=0)
 
 
 def contract_rows(left, right):
@@ -67,7 +72,7 @@
     dact_part = contract_cols(recv_dy, down_mat)
     gate, up, dact = (
         lax.psum(gate_part.astype(jnp.bfloat16), "tp").astype(jnp.float32),
-        lax.psum(up_part.astype(jnp.bfloat16), "tp").astype(jnp.float32),
+        add_all(up_part.astype(jnp.bfloat16), "tp").astype(jnp.float32),
         lax.psum(dact_part.astype(jnp.bfloat16), "tp").astype(jnp.float32),
     )
     act, dgate, dup = swiglu_back(gate, up, dact)

time: 203 us -> 197 us (0.970)
  blocking collectives: 0 us -> 36.1 us
  waiting for transfers between devices: 118 us -> 83.8 us
  starting transfers between devices: 16.6 us -> 9.97 us
  matrix products: 29.9 us -> 25.2 us
  other arithmetic: 5.5 us -> 8.52 us
    all_to_all x0 -> x1, blocking collectives: none -> 36.1 us  [on_device(): lax.all_to_all(send_x, 'ep', split_axis=0, concat_axis=0, tiled=True)]
    all_to_all x1 -> x0, waiting for transfers between devices: 21.6 us -> none  [on_device(): lax.all_to_all(send_x, 'ep', split_axis=0, concat_axis=0, tiled=True)]
    psum x1, waiting for transfers between devices: 59.7 us -> 41.9 us  [on_device(): lax.psum(dact_part.astype(jnp.bfloat16), 'tp').astype(jnp.float32)]
    all_to_all x1 -> x0, starting transfers between devices: 7.44 us -> none  [on_device(): lax.all_to_all(send_x, 'ep', split_axis=0, concat_axis=0, tiled=True)]
    all_to_all x1, waiting for transfers between devices: 21.6 us -> 25.7 us  [on_device(): lax.all_to_all(send_dy, 'ep', split_axis=0, concat_axis=0, tiled=True)]
    reduce_sum x0 -> x1, other arithmetic: none -> 3.03 us  [add_all(): return jnp.sum(blocks, axis=0)]
  transfers between devices with their start and end apart: 4 -> 4, of which waited for: 4 -> 3; matrix products, arithmetic and copies ran while one was open for 14% -> 14% of each run, Pallas kernels for 0% -> 0%
where the time goes in v1:
time: 197 us
  waiting for transfers between devices  83.8 us (43%)
  blocking collectives  36.1 us (18%)
  matrix products  25.2 us (13%)
  local copies, waits for them, and re-layouts  18.8 us (10%)
  between operations  14.3 us (7%)
  starting transfers between devices  9.97 us (5%)
  other arithmetic  8.52 us (4%)
    psum x1, waiting for transfers between devices, on_device(): lax.psum(dact_part.astype(jnp.bfloat16), 'tp').astype(jnp.float32)  41.9 us
    all_to_all x1, blocking collectives, on_device(): lax.all_to_all(send_x, 'ep', split_axis=0, concat_axis=0, tiled=True)  36.1 us
    all_to_all x1, waiting for transfers between devices, on_device(): lax.all_to_all(send_dy, 'ep', split_axis=0, concat_axis=0, tiled=True)  25.7 us
    all_to_all x1, waiting for transfers between devices, on_device(): lax.all_to_all(dx_rows.reshape(experts, capacity, width_part), 'ep', spli...  16.2 us
    dot_general x3, matrix products, contract_rows(): lax.dot_general(left, right, (((0,), (0,)), ((), ())), preferred_element_...  12.1 us
    dot_general x3, matrix products, contract_cols(): lax.dot_general(left, right, (((1,), (1,)), ((), ())), preferred_element_...  9.07 us
    all_to_all x1, starting transfers between devices, on_device(): lax.all_to_all(dx_rows.reshape(experts, capacity, width_part), 'ep', spli...  5.52 us
    all_to_all x1, starting transfers between devices, on_device(): lax.all_to_all(send_dy, 'ep', split_axis=0, concat_axis=0, tiled=True)  4.37 us
  transfers between devices with their start and end apart: 4, of which 3 were waited for; matrix products, arithmetic and copies ran while one was open for 14% of the time, Pallas kernels for 0%

profile of v1, /device:TPU:0, one launch (start us, length us, event | category | flops | bytes accessed | tf_op | source)
XLA Modules:
  0.0 196.8 jit_solution(5963182050243549084)
XLA Ops:
  7.2 0.8 broadcast_multiply_fusion
  8.0 0.8 copy.12
  9.0 0.1 copy.11
  9.1 0.1 mul.68
  9.3 1.1 reduce-window.6
  10.4 0.2 slice_reduce_fusion
  10.8 2.4 %scatter_custom_fusion = s32[576]{0:T(1024)S(1)} fusion(s32[512]{0:T(512)S(1)} %bitcast.55, s32[512]{0:T(512)S(1)} %iota.11, s32[]{:T(128)} %constant.15.clone.1), kind=kCustom, calls=%fused_computation.68 | custom fusion | bytes 2308 | tf_op jit(solution)/shard_map/scatter | solution.py:50
  13.3 1.0 concatenate.11
  14.2 2.9 %gather_fusion.2 = bf16[576,1024]{1,0:T(8,128)(2,1)S(1)} fusion(bf16[129,1024]{1,0:T(8,128)(2,1)S(1)} %concatenate.11, s32[1024]{0:T(1024)S(1)} %get-tuple-element.9), kind=kCustom, calls=%fused_computation.2 | custom fusion | bytes 2361600 | tf_op jit(solution)/shard_map/gather | solution.py:56
  17.1 36.1 %all_to_all.15 = bf16[8,72,1024]{2,1,0:T(8,128)(2,1)S(1)} all-to-all(bf16[8,72,1024]{2,1,0:T(8,128)(2,1)S(1)} %bitcast.48), channel_id=1, replica_groups=mesh['ep'=8,'tp'=4] {'ep'}, dimensions={0} | all-to-all | bytes 2359296 | tf_op jit(solution)/shard_map/all_to_all | solution.py:65
  53.3 1.0 copy-done.1
  54.3 2.0 %fusion.26 = bf16[576,768]{1,0:T(8,128)(2,1)} fusion(bf16[576,1024]{1,0:T(8,128)(2,1)S(1)} %bitcast.50, bf16[1,1024,768]{2,1,0:T(8,128)(2,1)S(1)} %copy-done.8), kind=kOutput, calls=%fused_computation.45 | convolution fusion | flops 906412032 | bytes 3637248 | tf_op jit(solution)/shard_map/dot_general | solution.py:71
  56.4 2.9 %gather_fusion = bf16[576,1024]{1,0:T(8,128)(2,1)S(1)} fusion(bf16[129,1024]{1,0:T(8,128)(2,1)S(1)} %concatenate.9, s32[1024]{0:T(1024)S(1)} %get-tuple-element.9), kind=kCustom, calls=%fused_computation | custom fusion | bytes 2361600 | tf_op jit(solution)/shard_map/gather | solution.py:57
  59.2 0.1 copy.14
  59.5 2.6 %gather_fusion.1 = f32[576]{0:T(1024)S(1)} fusion(f32[513]{0:T(1024)S(1)} %pad_maximum_fusion, s32[1024]{0:T(1024)S(1)} %get-tuple-element.8), kind=kCustom, calls=%fused_computation.1 | custom fusion | bytes 6912 | tf_op jit(solution)/shard_map/gather | solution.py:57
  62.1 1.3 fusion
  63.4 4.4 %all-to-all-start = ((bf16[8,72,1024]{2,1,0:T(8,128)(2,1)}), bf16[8,72,1024]{2,1,0:T(8,128)(2,1)}, u32[]{:S(2)}, u32[]{:S(2)}) async-start(bf16[8,72,1024]{2,1,0:T(8,128)(2,1)} %fusion), calls=%async_computation | async-start | bytes 2359296 | tf_op jit(solution)/shard_map/all_to_all | solution.py:66
  67.9 2.0 %fusion.29 = bf16[576,768]{1,0:T(8,128)(2,1)} fusion(bf16[576,1024]{1,0:T(8,128)(2,1)S(1)} %bitcast.52, bf16[1,1024,768]{2,1,0:T(8,128)(2,1)S(1)} %copy-done), kind=kOutput, calls=%fused_computation.46 | convolution fusion | flops 906412032 | bytes 3637248 | tf_op jit(solution)/shard_map/dot_general | solution.py:70
  69.9 25.7 %all-to-all-done = bf16[8,72,1024]{2,1,0:T(8,128)(2,1)} async-done(((bf16[8,72,1024]{2,1,0:T(8,128)(2,1)}), bf16[8,72,1024]{2,1,0:T(8,128)(2,1)}, u32[]{:S(2)}, u32[]{:S(2)}) %all-to-all-start) | async-done | bytes 1179680 | tf_op jit(solution)/shard_map/all_to_all | solution.py:66
  95.5 3.8 %fusion.23 = bf16[576,768]{1,0:T(8,128)(2,1)} fusion(bf16[576,1024]{1,0:T(8,128)(2,1)} %bitcast.5, bf16[1,768,1024]{2,1,0:T(8,128)(2,1)} %param.13), kind=kOutput, calls=%fused_computation.44 | convolution fusion | flops 906412032 | bytes 3637248 | tf_op jit(solution)/shard_map/dot_general | solution.py:19
  99.4 3.0 %reduce_sum.37 = bf16[576,768]{1,0:T(8,128)(2,1)S(1)} reduce(bf16[4,576,768]{2,1,0:T(8,128)(2,1)} %bitcast.49, bf16[]{:T(256)} %constant.14.clone.1), dimensions={0}, to_apply=%region_5.6 | reduce | flops 1327104 | bytes 4423682 | tf_op jit(solution)/shard_map/reduce_sum | solution.py:9
  102.5 41.9 %all-reduce.5.cloned.1.call-done = (bf16[576,768]{1,0:T(8,128)(2,1)}, bf16[576,768]{1,0:T(8,128)(2,1)}) async-done(((bf16[576,768]{1,0:T(8,128)(2,1)}, bf16[576,768]{1,0:T(8,128)(2,1)}), (bf16[576,768]{1,0:T(8,128)(2,1)}, bf16[576,768]{1,0:T(8,128)(2,1)})) %all-reduce.5.cloned.1.call-update) | async-done | bytes 1769488 | tf_op jit(solution)/shard_map/psum | solution.py:76
  144.4 3.1 %fusion.11 = f32[576,1024]{1,0:T(8,128)S(1)} fusion(bf16[1,1024,768]{2,1,0:T(8,128)(2,1)S(1)} %copy-done, bf16[576,768]{1,0:T(8,128)(2,1)S(1)} %reduce_sum.37, bf16[576,768]{1,0:T(8,128)(2,1)} %get-tuple-element.4, bf16[576,768]{1,0:T(8,128)(2,1)} %get-tuple-element.5), kind=kOutput, calls=%fused_computation.32 | convolution fusion | flops 911720448 | bytes 6586368 | tf_op jit(solution)/shard_map/dot_general | solution.py:19
  147.5 2.2 %add_convert_fusion = bf16[576,1024]{1,0:T(8,128)(2,1)} fusion(f32[576,1024]{1,0:T(8,128)S(1)} %fusion.11, bf16[1,1024,768]{2,1,0:T(8,128)(2,1)S(1)} %copy-done.9, bf16[576,768]{1,0:T(8,128)(2,1)S(1)} %copy-done.12, bf16[576,768]{1,0:T(8,128)(2,1)S(1)} %copy-done.10), kind=kOutput, calls=%fused_computation.16 | convolution fusion | flops 910688256 | bytes 6881280 | tf_op jit(solution)/shard_map/dot_general | solution.py:19
  149.7 5.5 %all-to-all-start.2 = ((bf16[8,72,1024]{2,1,0:T(8,128)(2,1)}), bf16[8,72,1024]{2,1,0:T(8,128)(2,1)S(1)}, u32[]{:S(2)}, u32[]{:S(2)}) async-start(bf16[8,72,1024]{2,1,0:T(8,128)(2,1)} %bitcast.54), calls=%async_computation.2 | async-start | bytes 2359296 | tf_op jit(solution)/shard_map/all_to_all | solution.py:80
  155.2 4.7 %fusion.21 = bf16[1,1024,768]{2,1,0:T(8,128)(2,1)} fusion(bf16[576,1024]{1,0:T(8,128)(2,1)} %bitcast.51, bf16[576,768]{1,0:T(8,128)(2,1)} %get-tuple-element.5, bf16[576,768]{1,0:T(8,128)(2,1)} %get-tuple-element.4), kind=kOutput, calls=%fused_computation.42 | convolution fusion | flops 914178048 | bytes 4521984 | tf_op jit(solution)/shard_map/dot_general | solution.py:13
  160.0 4.3 %fusion.22 = bf16[1,768,1024]{2,1,0:T(8,128)(2,1)} fusion(bf16[576,1024]{1,0:T(8,128)(2,1)} %bitcast.5, bf16[576,768]{1,0:T(8,128)(2,1)S(1)} %copy-done.5, bf16[576,768]{1,0:T(8,128)(2,1)S(1)} %copy-done.13), kind=kOutput, calls=%fused_computation.43 | convolution fusion | flops 914178048 | bytes 4521984 | tf_op jit(solution)/shard_map/dot_general | solution.py:13
  164.3 3.1 %fusion.20 = bf16[1,1024,768]{2,1,0:T(8,128)(2,1)} fusion(bf16[576,1024]{1,0:T(8,128)(2,1)S(1)} %bitcast.53, bf16[576,768]{1,0:T(8,128)(2,1)S(1)} %copy-done.5, bf16[576,768]{1,0:T(8,128)(2,1)S(1)} %copy-done.11, bf16[576,768]{1,0:T(8,128)(2,1)S(1)} %copy-done.13), kind=kOutput, calls=%fused_computation.41 | convolution fusion | flops 916389888 | bytes 5406720 | tf_op jit(solution)/shard_map/dot_general | solution.py:13
  167.4 16.2 %all-to-all-done.2 = bf16[8,72,1024]{2,1,0:T(8,128)(2,1)S(1)} async-done(((bf16[8,72,1024]{2,1,0:T(8,128)(2,1)}), bf16[8,72,1024]{2,1,0:T(8,128)(2,1)S(1)}, u32[]{:S(2)}, u32[]{:S(2)}) %all-to-all-start.2) | async-done | bytes 1179680 | tf_op jit(solution)/shard_map/all_to_all | solution.py:80
  183.6 2.8 %gather_fusion.3 = bf16[512,1024]{1,0:T(8,128)(2,1)} fusion(bf16[576,1024]{1,0:T(8,128)(2,1)S(1)} %bitcast.46, s32[1024]{0:T(1024)S(1)} %pad_clamp_fusion), kind=kCustom, calls=%fused_computation.3 | custom fusion | bytes 2099200 | tf_op jit(solution)/shard_map/gather | solution.py:92
  186.4 1.5 gather.18
  187.8 2.1 %reduce_sum.38 = bf16[128,1024]{1,0:T(8,128)(2,1)} reduce(bf16[128,4,1024]{2,1,0:T(4,128)(2,1)S(1)} %gather.18, bf16[]{:T(256)} %constant.14.clone.1), dimensions={1}, to_apply=%region_7.8 | reduce | flops 393216 | bytes 1310722 | tf_op jit(solution)/shard_map/reduce_sum | solution.py:93
  (47 shorter events, 0.8 us)
Async XLA Ops:
  7.2 60.7 %copy-start = (bf16[1,1024,768]{2,1,0:T(8,128)(2,1)S(1)}, bf16[1,1024,768]{2,1,0:T(8,128)(2,1)}, u32[]{:S(2)}) copy-start(bf16[1,1024,768]{2,1,0:T(8,128)(2,1)} %param.11) | copy-start | bytes 4718596
  7.2 92.2 %all-gather.3.cloned.1.call-start = ((), (), s32[]{:S(2)}) async-start(), calls=%async_computation.3 | async-start | bytes 4423680 | tf_op jit(solution)/shard_map/all_gather | solution.py:8
  17.1 37.2 %copy-start.8 = (bf16[1,1024,768]{2,1,0:T(8,128)(2,1)S(1)}, bf16[1,1024,768]{2,1,0:T(8,128)(2,1)}, u32[]{:S(2)}) copy-start(bf16[1,1024,768]{2,1,0:T(8,128)(2,1)} %param.12) | copy-start | bytes 4718596
  53.3 1.0 copy-start.1
  54.3 2.0 %copy-start.6 = (bf16[128,1024]{1,0:T(8,128)(2,1)S(1)}, bf16[128,1024]{1,0:T(8,128)(2,1)}, u32[]{:S(2)}) copy-start(bf16[128,1024]{1,0:T(8,128)(2,1)} %param.8) | copy-start | bytes 786436
  56.3 2.9 %copy-start.7 = (f32[128,4]{0,1:T(4,128)S(1)}, f32[128,4]{0,1:T(4,128)}, u32[]{:S(2)}) copy-start(f32[128,4]{0,1:T(4,128)} %param.10) | copy-start | bytes 6148
  63.4 4.4 %copy-start.2 = (bf16[8,72,1024]{2,1,0:T(8,128)(2,1)S(1)}, bf16[8,72,1024]{2,1,0:T(8,128)(2,1)}, u32[]{:S(2)}) copy-start(bf16[8,72,1024]{2,1,0:T(8,128)(2,1)} %copy-done.1) | copy-start | bytes 3538948
  63.4 32.1 %all-to-all-start = ((bf16[8,72,1024]{2,1,0:T(8,128)(2,1)}), bf16[8,72,1024]{2,1,0:T(8,128)(2,1)}, u32[]{:S(2)}, u32[]{:S(2)}) async-start(bf16[8,72,1024]{2,1,0:T(8,128)(2,1)} %fusion), calls=%async_computation | async-start | bytes 2359296 | tf_op jit(solution)/shard_map/all_to_all | solution.py:66
  67.8 76.6 %all-reduce.5.cloned.1.call-start = ((), (), s32[]{:S(2)}) async-start(), calls=%async_computation.4 | async-start | bytes 3538944 | tf_op jit(solution)/shard_map/psum | solution.py:76
  102.4 45.0 %copy-start.4 = (bf16[576,768]{1,0:T(8,128)(2,1)}, bf16[576,768]{1,0:T(8,128)(2,1)S(1)}, u32[]{:S(2)}) copy-start(bf16[576,768]{1,0:T(8,128)(2,1)S(1)} %reduce_sum.37) | copy-start | bytes 2654212
  144.4 3.1 %copy-start.9 = (bf16[1,1024,768]{2,1,0:T(8,128)(2,1)S(1)}, bf16[1,1024,768]{2,1,0:T(8,128)(2,1)}, u32[]{:S(2)}) copy-start(bf16[1,1024,768]{2,1,0:T(8,128)(2,1)} %param.12) | copy-start | bytes 4718596
  144.4 3.1 %copy-start.10 = (bf16[576,768]{1,0:T(8,128)(2,1)S(1)}, bf16[576,768]{1,0:T(8,128)(2,1)}, u32[]{:S(2)}) copy-start(bf16[576,768]{1,0:T(8,128)(2,1)} %get-tuple-element.4) | copy-start | bytes 2654212
  144.4 3.1 %copy-start.12 = (bf16[576,768]{1,0:T(8,128)(2,1)S(1)}, bf16[576,768]{1,0:T(8,128)(2,1)}, u32[]{:S(2)}) copy-start(bf16[576,768]{1,0:T(8,128)(2,1)} %get-tuple-element.5) | copy-start | bytes 2654212
  149.7 33.9 %all-to-all-start.2 = ((bf16[8,72,1024]{2,1,0:T(8,128)(2,1)}), bf16[8,72,1024]{2,1,0:T(8,128)(2,1)S(1)}, u32[]{:S(2)}, u32[]{:S(2)}) async-start(bf16[8,72,1024]{2,1,0:T(8,128)(2,1)} %bitcast.54), calls=%async_computation.2 | async-start | bytes 2359296 | tf_op jit(solution)/shard_map/all_to_all | solution.py:80
  155.2 4.7 %copy-start.5 = (bf16[576,768]{1,0:T(8,128)(2,1)S(1)}, bf16[576,768]{1,0:T(8,128)(2,1)}, u32[]{:S(2)}) copy-start(bf16[576,768]{1,0:T(8,128)(2,1)} %copy-done.4) | copy-start | bytes 2654212
  155.2 4.7 %copy-start.13 = (bf16[576,768]{1,0:T(8,128)(2,1)S(1)}, bf16[576,768]{1,0:T(8,128)(2,1)}, u32[]{:S(2)}) copy-start(bf16[576,768]{1,0:T(8,128)(2,1)} %get-tuple-element.5) | copy-start | bytes 2654212
  160.0 4.4 %copy-start.3 = (bf16[8,72,1024]{2,1,0:T(8,128)(2,1)S(1)}, bf16[8,72,1024]{2,1,0:T(8,128)(2,1)}, u32[]{:S(2)}) copy-start(bf16[8,72,1024]{2,1,0:T(8,128)(2,1)} %copy-done.1) | copy-start | bytes 3538948
  160.0 4.4 %copy-start.11 = (bf16[576,768]{1,0:T(8,128)(2,1)S(1)}, bf16[576,768]{1,0:T(8,128)(2,1)}, u32[]{:S(2)}) copy-start(bf16[576,768]{1,0:T(8,128)(2,1)} %get-tuple-element.4) | copy-start | bytes 2654212
Sparse Core Ops, SparseCore 0:
  56.4 29.4 all-gather.2
  99.5 44.8 all-reduce.4
